TPU v7x, 256 devices: a whole 4x4x8 slice. The times are simulated.
256 devices in a mesh: dp: 4 (over y), graph: 64 (over z, x, core).
Axes of the slice: x: 4, y: 4, z: 8, core: 2. Of those that a mesh axis runs over, the one named last changes fastest.
Arguments:
- edge_state: bfloat16 [4, 131072, 512], P('dp', 'graph'), may hold values from -6 to 6
- cotangent: bfloat16 [4, 131072, 512], P('dp', 'graph'), may hold values from -6 to 6
- edge_count: int32 [4, 64], P('dp', 'graph'), may hold values from 1024 to 2048, as said below
- triplet_basis: bfloat16 [4, 16, 524288], P('dp', None, 'graph'), may hold values from -6 to 6
- triplet_in: int32 [4, 524288], P('dp', 'graph'), may hold values from 0 to 2047, as said below
- triplet_out: int32 [4, 524288], P('dp', 'graph'), may hold values from 0 to 2047, as said below
- down_weight: bfloat16 [512, 64], replicated, may hold values from -0.25 to 0.25
- basis_weight: bfloat16 [16, 64], replicated, may hold values from -1.5 to 1.5
- bilinear_weight: bfloat16 [64, 64], replicated, may hold values from -0.75 to 0.75
- up_weight: bfloat16 [64, 512], replicated, may hold values from -0.75 to 0.75
- first_weight: bfloat16 [512, 512], replicated, may hold values from -0.25 to 0.25
- second_weight: bfloat16 [512, 512], replicated, may hold values from -0.25 to 0.25
Outputs:
- edge_grad: bfloat16 [4, 131072, 512], P('dp', 'graph')
- down_grad: float32 [512, 64], replicated
- basis_grad: float32 [16, 64], replicated
- bilinear_grad: float32 [64, 64], replicated
- up_grad: float32 [64, 512], replicated
- first_grad: float32 [512, 512], replicated
- second_grad: float32 [512, 512], replicated
Inputs may be any that keep to these rules, and one draw needn't show every extreme that they name: `edge_count`: every entry is a multiple of 128; in every batch some shard holds all 2048 slots live. Slot s * 8192 + j * 128 + k (s and j below 64, k below 128) holds a triplet of shard s whose in-edge is row triplet_in of shard j, a live row: below edge_count[b, j]. Slot s * 8192 + t holds a triplet whose out-edge is row triplet_out of shard s, a live row: below edge_count[b, s].
All inputs are finite; a program needn't handle non-finite values.
Results may differ from a plain program's by a relative error of at most 0.0096.
Values may be sent and summed in bfloat16 or wider, within the bound.
A program may use at most 128 MiB of HBM per device.

v0:
```python
import math
import jax
import jax.numpy as jnp
from jax import lax
from jax.sharding import PartitionSpec as P

HALF = 0.7071067811865476


def silu_slope(argument):
    logistic = jax.nn.sigmoid(argument)
    return logistic * (1.0 + argument * (1.0 - logistic))


def contract(left, right, left_dim, right_dim):
    return lax.dot_general(
        left, right, (((left_dim,), (right_dim,)), ((), ())), preferred_element_type=jnp.float32
    )


def local(
    edge_state,
    cotangent,
    edge_count,
    triplet_basis,
    triplet_in,
    triplet_out,
    down_weight,
    basis_weight,
    bilinear_weight,
    up_weight,
    first_weight,
    second_weight,
):
    edge_rows = edge_state[0]
    row_count = edge_rows.shape[0]
    shards = lax.axis_size("graph")
    narrow = down_weight.shape[1]
    in_local = triplet_in[0]
    out_local = triplet_out[0]
    tri_rows = in_local.shape[0]
    slot_count = tri_rows // shards
    live_mask = (jnp.arange(row_count, dtype=jnp.int32) < edge_count[0, 0]).astype(jnp.float32)
    wanted = lax.all_to_all(
        in_local.reshape(shards, slot_count), "graph", split_axis=0, concat_axis=0, tiled=True
    ).reshape(tri_rows)
    pre_down = contract(down_weight, edge_rows, 0, 1)
    down_rows = jax.nn.silu(pre_down).astype(jnp.bfloat16)
    tri_coef = contract(basis_weight, triplet_basis[0], 0, 0)
    served = jnp.take(down_rows, wanted, axis=1).reshape(narrow, shards, slot_count)
    fetched = lax.all_to_all(served, "graph", split_axis=1, concat_axis=1, tiled=True).reshape(
        narrow, tri_rows
    )
    message = tri_coef * fetched.astype(jnp.float32)
    gathered = (
        jnp.zeros((narrow, row_count), jnp.float32)
        .at[:, out_local]
        .add(message)
        .astype(jnp.bfloat16)
    )
    mixed_rows = contract(bilinear_weight, gathered, 0, 0).astype(jnp.bfloat16)
    pre_up = contract(mixed_rows, up_weight, 0, 0)
    summed = edge_rows.astype(jnp.float32) + jax.nn.silu(pre_up)
    summed_half = summed.astype(jnp.bfloat16)
    pre_first = jnp.dot(summed_half, first_weight, preferred_element_type=jnp.float32)
    first_rows = jax.nn.silu(pre_first).astype(jnp.bfloat16)
    pre_second = jnp.dot(first_rows, second_weight, preferred_element_type=jnp.float32)
    back_top = cotangent[0].astype(jnp.float32) * live_mask[:, None] * HALF
    back_second = (back_top * silu_slope(pre_second)).astype(jnp.bfloat16)
    back_first = (contract(back_second, second_weight, 1, 1) * silu_slope(pre_first)).astype(
        jnp.bfloat16
    )
    first_grad = contract(summed_half, back_first, 0, 0)
    second_grad = contract(first_rows, back_second, 0, 0)
    back_summed = back_top + contract(back_first, first_weight, 1, 1)
    back_up = (back_summed * silu_slope(pre_up)).astype(jnp.bfloat16)
    back_mixed = contract(up_weight, back_up, 1, 1).astype(jnp.bfloat16)
    back_gathered = contract(bilinear_weight, back_mixed, 1, 0)
    back_message = jnp.take(back_gathered, out_local, axis=1)
    back_coef = (back_message * fetched.astype(jnp.float32)).astype(jnp.bfloat16)
    back_fetched = back_message * tri_coef
    returned = (
        lax.all_to_all(
            back_fetched.reshape(narrow, shards, slot_count).astype(jnp.bfloat16),
            "graph",
            split_axis=1,
            concat_axis=1,
            tiled=True,
        )
        .astype(jnp.float32)
        .reshape(narrow, tri_rows)
    )
    back_down = jnp.zeros((narrow, row_count), jnp.float32).at[:, wanted].add(returned)
    up_grad = contract(mixed_rows, back_up, 1, 0)
    bilinear_grad = contract(gathered, back_mixed, 1, 1)
    basis_grad = contract(triplet_basis[0], back_coef, 1, 1)
    back_pre = (back_down * silu_slope(pre_down)).astype(jnp.bfloat16)
    down_grad = contract(edge_rows, back_pre, 0, 1)
    edge_grad = (back_summed + contract(back_pre, down_weight, 0, 1)).astype(jnp.bfloat16)
    down_grad, basis_grad, bilinear_grad, up_grad, first_grad, second_grad = lax.psum(
        (down_grad, basis_grad, bilinear_grad, up_grad, first_grad, second_grad), ("dp", "graph")
    )
    grad_scale = 1.0 / math.sqrt(lax.axis_size("dp") * shards * row_count)
    return (
        edge_grad[None],
        down_grad * grad_scale,
        basis_grad * grad_scale,
        bilinear_grad * grad_scale,
        up_grad * grad_scale,
        first_grad * grad_scale,
        second_grad * grad_scale,
    )


def solution(mesh):
    in_specs = (
        P("dp", "graph", None),
        P("dp", "graph", None),
        P("dp", "graph"),
        P("dp", None, "graph"),
        P("dp", "graph"),
        P("dp", "graph"),
        P(),
        P(),
        P(),
        P(),
        P(),
        P(),
    )
    out_specs = (P("dp", "graph", None), P(), P(), P(), P(), P(), P())
    return jax.shard_map(local, mesh=mesh, in_specs=in_specs, out_specs=out_specs, check_vma=False)
```

profile of v0, /device:TPU:2, one launch (start us, length us, event | category | flops | bytes accessed | tf_op | source)
XLA Modules:
  0.0 558.6 jit_solution(4663164017009512426)
XLA Ops:
  7.2 12.2 %all-to-all-start = ((s32[64,1,128]{2,1,0:T(1,128)}), s32[64,1,128]{2,1,0:T(1,128)S(1)}, u32[]{:S(2)}, u32[]{:S(2)}) async-start(s32[64,1,128]{2,1,0:T(1,128)} %bitcast.127), calls=%async_computation | async-start | bytes 65536 | tf_op jit(solution)/shard_map/all_to_all | solution.py:44
  20.0 0.8 compare_and_fusion.1
  20.8 3.2 multiply_convert_fusion.4
  24.3 3.6 all-to-all-done
  28.0 24.0 %gather_fusion = bf16[8192,64]{1,0:T(8,128)(2,1)S(1)} fusion(bf16[64,2048]{0,1:T(8,128)(2,1)S(1)} %copy.35, s32[8192]{0:T(1024)S(1)} %broadcast_clamp_fusion.1), kind=kCustom, calls=%fused_computation | custom fusion | bytes 2129920 | tf_op jit(solution)/shard_map/jit(_take)/gather | solution.py:50
  52.0 1.6 copy.36
  53.6 2.4 broadcast_select_fusion
  56.0 6.9 %all-to-all-start.1 = ((bf16[64,64,128]{2,0,1:T(8,128)(2,1)}), bf16[64,64,128]{2,0,1:T(8,128)(2,1)}, u32[]{:S(2)}, u32[]{:S(2)}) async-start(bf16[64,64,128]{2,0,1:T(8,128)(2,1)} %broadcast_select_fusion), calls=%async_computation.1 | async-start | bytes 2097152 | tf_op jit(solution)/shard_map/all_to_all | solution.py:51
  63.0 0.4 fusion.25
  63.4 28.1 %all-to-all-done.1 = bf16[64,64,128]{2,0,1:T(8,128)(2,1)} async-done(((bf16[64,64,128]{2,0,1:T(8,128)(2,1)}), bf16[64,64,128]{2,0,1:T(8,128)(2,1)}, u32[]{:S(2)}, u32[]{:S(2)}) %all-to-all-start.1) | async-done | bytes 1048608 | tf_op jit(solution)/shard_map/all_to_all | solution.py:51
  91.5 2.7 fusion.6
  94.3 3.8 copy.38
  98.1 45.3 %scatter_custom_fusion = f32[64,2048]{0,1:T(8,128)} fusion(s32[8192]{0:T(1024)S(1)} %bitcast.126, f32[8192,64]{1,0:T(8,128)} %copy.38, f32[]{:T(128)} %constant.18.clone.1), kind=kCustom, calls=%fused_computation.50 | custom fusion | flops 524288 | bytes 524800 | tf_op jit(solution)/shard_map/scatter-add | solution.py:58
  143.4 1.5 convolution_convert_fusion.1
  144.9 2.9 add_convert_fusion.1
  147.9 1.9 multiply_convert_fusion.2
  149.8 0.4 copy-done.14
  150.3 2.6 fusion.3
  152.9 2.3 multiply_convert_fusion.1
  155.3 4.0 multiply_convert_fusion
  159.2 0.7 convolution_convert_fusion
  160.0 0.6 copy-done.4
  160.6 0.7 copy-done.6
  161.3 1.0 convolution_bitcast_fusion
  162.3 1.4 copy.39
  163.6 27.9 %gather_fusion.1 = f32[8192,64]{1,0:T(8,128)} fusion(f32[64,2048]{0,1:T(8,128)S(1)} %copy.39, s32[8192]{0:T(1024)S(1)} %broadcast_clamp_fusion), kind=kCustom, calls=%fused_computation.1 | custom fusion | bytes 4227072 | tf_op jit(solution)/shard_map/jit(_take)/gather | solution.py:79
  191.6 3.8 copy.40
  195.3 2.9 copy_bitcast_fusion
  198.2 5.8 %all-to-all-start.2 = ((bf16[64,64,128]{2,0,1:T(8,128)(2,1)}), bf16[64,64,128]{2,0,1:T(8,128)(2,1)S(1)}, u32[]{:S(2)}, u32[]{:S(2)}) async-start(bf16[64,64,128]{2,0,1:T(8,128)(2,1)} %copy_bitcast_fusion), calls=%async_computation.2 | async-start | bytes 2097152 | tf_op jit(solution)/shard_map/all_to_all | solution.py:83
  204.4 1.1 fusion.31
  205.5 0.5 copy-done.21
  206.0 4.0 fusion.33
  210.0 2.3 fusion.32
  212.3 20.6 %all-to-all-done.2 = bf16[64,64,128]{2,0,1:T(8,128)(2,1)S(1)} async-done(((bf16[64,64,128]{2,0,1:T(8,128)(2,1)}), bf16[64,64,128]{2,0,1:T(8,128)(2,1)S(1)}, u32[]{:S(2)}, u32[]{:S(2)}) %all-to-all-start.2) | async-done | bytes 1048608 | tf_op jit(solution)/shard_map/all_to_all | solution.py:83
  233.0 2.8 copy.43
  235.8 44.6 %scatter_custom_fusion.1 = f32[64,2048]{0,1:T(8,128)S(1)} fusion(s32[8192]{0:T(1024)S(1)} %bitcast.124, f32[8192,64]{1,0:T(8,128)} %copy.43, f32[]{:T(128)} %constant.18.clone.1), kind=kCustom, calls=%fused_computation.48 | custom fusion | flops 524288 | bytes 524800 | tf_op jit(solution)/shard_map/scatter-add | solution.py:93
  280.4 0.3 copy.44
  280.9 2.8 fusion.13
  283.8 1.4 fusion.27
  285.4 1.7 convolution_bitcast_fusion.1
  287.1 74.4 %all-reduce = (f32[16,64]{1,0:T(8,128)S(1)}, f32[64,64]{1,0:T(8,128)S(1)}) all-reduce(f32[16,64]{1,0:T(8,128)S(1)} %convolution_bitcast_fusion.1, f32[64,64]{1,0:T(8,128)S(1)} %fusion.27), channel_id=1, replica_groups=mesh['dp'=4,'graph'=64] {'dp','graph'}, use_global_device_ids=true, to_apply=%region_3.4 | all-reduce | flops 5120 | bytes 40960 | tf_op jit(solution)/shard_map/psum | solution.py:100
  361.5 0.6 broadcast_multiply_fusion.5
  362.1 0.6 broadcast_multiply_fusion.4
  362.7 4.3 fusion.4
  367.0 178.4 %all-reduce.4.cloned.1.call-done = (f32[512,64]{0,1:T(8,128)}, f32[64,512]{1,0:T(8,128)}, f32[512,512]{1,0:T(8,128)}, f32[512,512]{1,0:T(8,128)}) async-done(((f32[512,64]{0,1:T(8,128)}, f32[64,512]{1,0:T(8,128)}, f32[512,512]{1,0:T(8,128)}, f32[512,512]{1,0:T(8,128)}), (f32[512,64]{0,1:T(8,128)}, f32[64,512]{1,0:T(8,128)}, f32[512,512]{1,0:T(8,128)}, f32[512,512]{1,0:T(8,128)})) %all-reduce.4.cloned.1.call-update) | async-done | bytes 2359312 | tf_op jit(solution)/shard_map/psum | solution.py:100
  545.4 1.6 broadcast_multiply_fusion.3
  547.0 1.6 broadcast_multiply_fusion.2
  548.6 3.2 broadcast_multiply_fusion
  (54 shorter events, 1.4 us)
Async XLA Ops:
  7.2 140.7 %copy-start = (bf16[512,512]{1,0:T(8,128)(2,1)S(1)}, bf16[512,512]{1,0:T(8,128)(2,1)}, u32[]{:S(2)}) copy-start(bf16[512,512]{1,0:T(8,128)(2,1)} %param.22) | copy-start | bytes 1572868
  7.2 20.7 %all-to-all-start = ((s32[64,1,128]{2,1,0:T(1,128)}), s32[64,1,128]{2,1,0:T(1,128)S(1)}, u32[]{:S(2)}, u32[]{:S(2)}) async-start(s32[64,1,128]{2,1,0:T(1,128)} %bitcast.127), calls=%async_computation | async-start | bytes 65536 | tf_op jit(solution)/shard_map/all_to_all | solution.py:44
  53.6 9.2 %copy-start.8 = (s32[1,8192]{1,0:T(1,128)S(1)}, s32[1,8192]{1,0:T(1,128)}, u32[]{:S(2)}) copy-start(s32[1,8192]{1,0:T(1,128)} %param.17) | copy-start | bytes 98308
  53.6 9.3 %copy-start.9 = (bf16[1,16,8192]{2,1,0:T(8,128)(2,1)S(1)}, bf16[1,16,8192]{2,1,0:T(8,128)(2,1)}, u32[]{:S(2)}) copy-start(bf16[1,16,8192]{2,1,0:T(8,128)(2,1)} %param.15) | copy-start | bytes 786436
  53.6 9.3 %copy-start.13 = (bf16[16,64]{1,0:T(8,128)(2,1)S(1)}, bf16[16,64]{1,0:T(8,128)(2,1)}, u32[]{:S(2)}) copy-start(bf16[16,64]{1,0:T(8,128)(2,1)} %param.19) | copy-start | bytes 6148
  56.0 35.6 %all-to-all-start.1 = ((bf16[64,64,128]{2,0,1:T(8,128)(2,1)}), bf16[64,64,128]{2,0,1:T(8,128)(2,1)}, u32[]{:S(2)}, u32[]{:S(2)}) async-start(bf16[64,64,128]{2,0,1:T(8,128)(2,1)} %broadcast_select_fusion), calls=%async_computation.1 | async-start | bytes 2097152 | tf_op jit(solution)/shard_map/all_to_all | solution.py:51
  94.3 49.1 %copy-start.12 = (bf16[64,64]{1,0:T(8,128)(2,1)S(1)}, bf16[64,64]{1,0:T(8,128)(2,1)}, u32[]{:S(2)}) copy-start(bf16[64,64]{1,0:T(8,128)(2,1)} %param.20) | copy-start | bytes 24580
  98.1 46.9 %copy-start.11 = (bf16[64,512]{1,0:T(8,128)(2,1)S(1)}, bf16[64,512]{1,0:T(8,128)(2,1)}, u32[]{:S(2)}) copy-start(bf16[64,512]{1,0:T(8,128)(2,1)} %param.21) | copy-start | bytes 196612
  147.8 1.9 copy-start.16
  147.8 2.3 copy-start.14
  147.9 2.4 copy-start.15
  149.8 3.1 copy-start.20
  152.9 2.3 copy-start.22
  155.2 4.0 copy-start.18
  159.2 1.3 copy-start.4
  160.6 0.7 copy-start.6
  198.2 6.1 %copy-start.5 = (bf16[2048,512]{1,0:T(8,128)(2,1)S(1)}, bf16[2048,512]{1,0:T(8,128)(2,1)}, u32[]{:S(2)}) copy-start(bf16[2048,512]{1,0:T(8,128)(2,1)} %copy-done.4) | copy-start | bytes 6291460
  198.2 34.6 %all-to-all-start.2 = ((bf16[64,64,128]{2,0,1:T(8,128)(2,1)}), bf16[64,64,128]{2,0,1:T(8,128)(2,1)S(1)}, u32[]{:S(2)}, u32[]{:S(2)}) async-start(bf16[64,64,128]{2,0,1:T(8,128)(2,1)} %copy_bitcast_fusion), calls=%async_computation.2 | async-start | bytes 2097152 | tf_op jit(solution)/shard_map/all_to_all | solution.py:83
  204.0 341.4 %all-reduce.4.cloned.1.call-start = ((), (), s32[]{:S(2)}) async-start(), calls=%async_computation.3 | async-start | bytes 4718592 | tf_op jit(solution)/shard_map/psum | solution.py:100
  204.3 1.6 copy-start.21
  206.0 4.0 copy-start.17
  206.0 4.0 copy-start.19
  235.8 44.9 %copy-start.7 = (f32[64,2048]{1,0:T(8,128)S(1)}, f32[64,2048]{1,0:T(8,128)}, u32[]{:S(2)}) copy-start(f32[64,2048]{1,0:T(8,128)} %get-tuple-element.14) | copy-start | bytes 1572868
  280.9 2.9 copy-start.2
  283.7 1.7 copy-start.3
  285.4 77.3 %copy-start.10 = (bf16[512,64]{0,1:T(8,128)(2,1)S(1)}, bf16[512,64]{0,1:T(8,128)(2,1)}, u32[]{:S(2)}) copy-start(bf16[512,64]{0,1:T(8,128)(2,1)} %param.18) | copy-start | bytes 196612
  548.6 3.2 copy-start.1
Sparse Core Ops, SparseCore 0:
  283.9 261.4 all-reduce.3
where the time goes:
time: 560 us; the launch traced here: 559 us
  waiting for transfers between devices  231 us (41%)
  other arithmetic  107 us (19%)
  blocking collectives  74.4 us (13%)
  local copies, waits for them, and re-layouts  68.5 us (12%)
  matrix products  38.2 us (7%)
  starting transfers between devices  25.1 us (4%)
  between operations  15 us (3%)
    psum x1, waiting for transfers between devices, local(): lax.psum((down_grad, basis_grad, bilinear_grad, up_grad, first_grad, seco...  178 us
    psum x1, blocking collectives, local(): lax.psum((down_grad, basis_grad, bilinear_grad, up_grad, first_grad, seco...  74.4 us
    scatter-add x1, other arithmetic, local(): gathered = jnp.zeros((narrow, row_count), jnp.float32).at[:, out_local].a...  45.3 us
    scatter-add x1, other arithmetic, local(): jnp.zeros((narrow, row_count), jnp.float32).at[:, wanted].add(returned)  44.6 us
    dot_general x15, matrix products, contract(): lax.dot_general(left, right, (((left_dim,), (right_dim,)), ((), ())), pre...  33.7 us
    gather x2, local copies, waits for them, and re-layouts, local(): back_message = jnp.take(back_gathered, out_local, axis=1)  31.7 us
    all_to_all x1, waiting for transfers between devices, local(): lax.all_to_all(served, 'graph', split_axis=1, concat_axis=1, tiled=True)  28.1 us
    gather x2, local copies, waits for them, and re-layouts, local(): jnp.take(down_rows, wanted, axis=1).reshape(narrow, shards, slot_count)  25.6 us
  transfers between devices with their start and end apart: 4, of which 4 were waited for; matrix products, arithmetic and copies ran while one was open for 4% of the time, Pallas kernels for 0%

commit v1 on v0

--- a/solution.py
+++ b/solution.py
@@ -98,7 +98,8 @@
     down_grad = contract(edge_rows, back_pre, 0, 1)
     edge_grad = (back_summed + contract(back_pre, down_weight, 0, 1)).astype(jnp.bfloat16)
     down_grad, basis_grad, bilinear_grad, up_grad, first_grad, second_grad = lax.psum(
-        (down_grad, basis_grad, bilinear_grad, up_grad, first_grad, second_grad), ("dp", "graph")
+        lax.psum((down_grad, basis_grad, bilinear_grad, up_grad, first_grad, second_grad), "graph"),
+        "dp",
     )
     grad_scale = 1.0 / math.sqrt(lax.axis_size("dp") * shards * row_count)
     return (

time: 560 us -> 760 us (1.36)
  blocking collectives: 74.4 us -> 262 us
  waiting for transfers between devices: 231 us -> 240 us
    psum x1, blocking collectives: 74.4 us -> 245 us  [local(): lax.psum((down_grad, basis_grad, bilinear_grad, up_grad, first_grad, seco...]
    psum x0 -> x1, blocking collectives: none -> 17.3 us  [local(): lax.psum(lax.psum((down_grad, basis_grad, bilinear_grad, up_grad, first_g...]
    psum x1, waiting for transfers between devices: 178 us -> 188 us  [local(): lax.psum((down_grad, basis_grad, bilinear_grad, up_grad, first_grad, seco...]
  transfers between devices with their start and end apart: 4 -> 5, of which waited for: 4 -> 4; matrix products, arithmetic and copies ran while one was open for 4% -> 3% of each run, Pallas kernels for 0% -> 0%
where the time goes in v1:
time: 760 us; the launch traced here: 755 us
  blocking collectives  262 us (34%)
  waiting for transfers between devices  240 us (32%)
  other arithmetic  107 us (14%)
  local copies, waits for them, and re-layouts  68.3 us (9%)
  matrix products  37.9 us (5%)
  starting transfers between devices  25.1 us (3%)
  between operations  15.1 us (2%)
    psum x1, blocking collectives, local(): lax.psum((down_grad, basis_grad, bilinear_grad, up_grad, first_grad, seco...  245 us
    psum x1, waiting for transfers between devices, local(): lax.psum((down_grad, basis_grad, bilinear_grad, up_grad, first_grad, seco...  188 us
    scatter-add x1, other arithmetic, local(): gathered = jnp.zeros((narrow, row_count), jnp.float32).at[:, out_local].a...  45.3 us
    scatter-add x1, other arithmetic, local(): jnp.zeros((narrow, row_count), jnp.float32).at[:, wanted].add(returned)  44.6 us
    dot_general x15, matrix products, contract(): lax.dot_general(left, right, (((left_dim,), (right_dim,)), ((), ())), pre...  33.4 us
    gather x2, local copies, waits for them, and re-layouts, local(): back_message = jnp.take(back_gathered, out_local, axis=1)  31.7 us
    all_to_all x1, waiting for transfers between devices, local(): lax.all_to_all(served, 'graph', split_axis=1, concat_axis=1, tiled=True)  28.1 us
    gather x2, local copies, waits for them, and re-layouts, local(): jnp.take(down_rows, wanted, axis=1).reshape(narrow, shards, slot_count)  25.6 us
  transfers between devices with their start and end apart: 5, of which 4 were waited for; matrix products, arithmetic and copies ran while one was open for 3% of the time, Pallas kernels for 0%

profile of v1, /device:TPU:2, one launch (start us, length us, event | category | flops | bytes accessed | tf_op | source)
XLA Modules:
  0.0 755.3 jit_solution(9274414857364310888)
XLA Ops:
  7.2 12.2 %all-to-all-start = ((s32[64,1,128]{2,1,0:T(1,128)}), s32[64,1,128]{2,1,0:T(1,128)S(1)}, u32[]{:S(2)}, u32[]{:S(2)}) async-start(s32[64,1,128]{2,1,0:T(1,128)} %bitcast.127), calls=%async_computation | async-start | bytes 65536 | tf_op jit(solution)/shard_map/all_to_all | solution.py:44
  20.0 0.8 compare_and_fusion.1
  20.8 3.2 multiply_convert_fusion.4
  24.3 3.6 all-to-all-done
  28.0 24.0 %gather_fusion = bf16[8192,64]{1,0:T(8,128)(2,1)S(1)} fusion(bf16[64,2048]{0,1:T(8,128)(2,1)S(1)} %copy.35, s32[8192]{0:T(1024)S(1)} %broadcast_clamp_fusion.1), kind=kCustom, calls=%fused_computation | custom fusion | bytes 2129920 | tf_op jit(solution)/shard_map/jit(_take)/gather | solution.py:50
  52.0 1.6 copy.36
  53.6 2.4 broadcast_select_fusion
  56.0 6.9 all-to-all-start.1
  63.0 0.4 fusion.25
  63.4 28.1 %all-to-all-done.1 = bf16[64,64,128]{2,0,1:T(8,128)(2,1)} async-done(((bf16[64,64,128]{2,0,1:T(8,128)(2,1)}), bf16[64,64,128]{2,0,1:T(8,128)(2,1)}, u32[]{:S(2)}, u32[]{:S(2)}) %all-to-all-start.1) | async-done | bytes 1048608 | tf_op jit(solution)/shard_map/all_to_all | solution.py:51
  91.5 2.7 fusion.6
  94.3 3.8 copy.38
  98.1 45.3 %scatter_custom_fusion = f32[64,2048]{0,1:T(8,128)} fusion(s32[8192]{0:T(1024)S(1)} %bitcast.126, f32[8192,64]{1,0:T(8,128)} %copy.38, f32[]{:T(128)} %constant.18.clone.1), kind=kCustom, calls=%fused_computation.50 | custom fusion | flops 524288 | bytes 524800 | tf_op jit(solution)/shard_map/scatter-add | solution.py:58
  143.4 1.5 convolution_convert_fusion.1
  144.9 2.9 add_convert_fusion.1
  147.9 1.9 multiply_convert_fusion.2
  149.8 0.4 copy-done.14
  150.3 2.6 fusion.3
  152.9 2.3 multiply_convert_fusion.1
  155.3 4.0 multiply_convert_fusion
  159.2 0.7 convolution_convert_fusion
  160.0 0.6 copy-done.4
  160.6 0.7 copy-done.6
  161.3 1.0 convolution_bitcast_fusion
  162.3 1.4 copy.39
  163.6 27.9 %gather_fusion.1 = f32[8192,64]{1,0:T(8,128)} fusion(f32[64,2048]{0,1:T(8,128)S(1)} %copy.39, s32[8192]{0:T(1024)S(1)} %broadcast_clamp_fusion), kind=kCustom, calls=%fused_computation.1 | custom fusion | bytes 4227072 | tf_op jit(solution)/shard_map/jit(_take)/gather | solution.py:79
  191.6 3.8 copy.40
  195.3 2.9 copy_bitcast_fusion
  198.2 5.8 all-to-all-start.2
  204.3 1.1 fusion.31
  205.5 0.5 copy-done.21
  206.0 4.0 fusion.33
  210.0 2.3 fusion.32
  212.3 20.6 %all-to-all-done.2 = bf16[64,64,128]{2,0,1:T(8,128)(2,1)S(1)} async-done(((bf16[64,64,128]{2,0,1:T(8,128)(2,1)}), bf16[64,64,128]{2,0,1:T(8,128)(2,1)S(1)}, u32[]{:S(2)}, u32[]{:S(2)}) %all-to-all-start.2) | async-done | bytes 1048608 | tf_op jit(solution)/shard_map/all_to_all | solution.py:83
  233.0 2.8 copy.43
  235.8 44.6 %scatter_custom_fusion.1 = f32[64,2048]{0,1:T(8,128)S(1)} fusion(s32[8192]{0:T(1024)S(1)} %bitcast.124, f32[8192,64]{1,0:T(8,128)} %copy.43, f32[]{:T(128)} %constant.18.clone.1), kind=kCustom, calls=%fused_computation.48 | custom fusion | flops 524288 | bytes 524800 | tf_op jit(solution)/shard_map/scatter-add | solution.py:93
  280.9 2.7 fusion.13
  283.7 187.8 %all-reduce.7.cloned.1.call-done = (f32[512,64]{0,1:T(8,128)}, f32[64,512]{1,0:T(8,128)}, f32[512,512]{1,0:T(8,128)}, f32[512,512]{1,0:T(8,128)}) async-done(((f32[512,64]{0,1:T(8,128)}, f32[64,512]{1,0:T(8,128)}, f32[512,512]{1,0:T(8,128)}, f32[512,512]{1,0:T(8,128)}), (f32[512,64]{0,1:T(8,128)}, f32[64,512]{1,0:T(8,128)}, f32[512,512]{1,0:T(8,128)}, f32[512,512]{1,0:T(8,128)})) %all-reduce.7.cloned.1.call-update) | async-done | bytes 2359312 | tf_op jit(solution)/shard_map/psum | solution.py:101
  471.6 1.2 fusion.27
  472.8 1.7 convolution_bitcast_fusion.1
  474.5 244.8 %all-reduce = (f32[16,64]{1,0:T(8,128)S(1)}, f32[64,64]{1,0:T(8,128)S(1)}) all-reduce(f32[16,64]{1,0:T(8,128)S(1)} %convolution_bitcast_fusion.1, f32[64,64]{1,0:T(8,128)S(1)} %fusion.27), channel_id=1, replica_groups=mesh['dp'=4,'graph'=64] {'graph'}, use_global_device_ids=true, to_apply=%region_4.5 | all-reduce | flops 5120 | bytes 40960 | tf_op jit(solution)/shard_map/psum | solution.py:101
  719.3 17.3 %all-reduce.2 = (f32[16,64]{1,0:T(8,128)S(1)}, f32[64,64]{1,0:T(8,128)S(1)}) all-reduce(f32[16,64]{1,0:T(8,128)S(1)} %get-tuple-element.7, f32[64,64]{1,0:T(8,128)S(1)} %get-tuple-element.8), channel_id=1, replica_groups=mesh['dp'=4,'graph'=64] {'dp'}, use_global_device_ids=true, to_apply=%region_5.6 | all-reduce | flops 5120 | bytes 40960 | tf_op jit(solution)/shard_map/psum | solution.py:100
  736.7 0.6 broadcast_multiply_fusion.5
  737.3 0.6 broadcast_multiply_fusion.4
  737.9 4.2 fusion.4
  742.2 1.6 broadcast_multiply_fusion.3
  743.7 1.6 broadcast_multiply_fusion.2
  745.3 3.2 broadcast_multiply_fusion
  (58 shorter events, 1.6 us)
Async XLA Ops:
  7.2 140.7 %copy-start = (bf16[512,512]{1,0:T(8,128)(2,1)S(1)}, bf16[512,512]{1,0:T(8,128)(2,1)}, u32[]{:S(2)}) copy-start(bf16[512,512]{1,0:T(8,128)(2,1)} %param.22) | copy-start | bytes 1572868
  7.2 20.7 %all-to-all-start = ((s32[64,1,128]{2,1,0:T(1,128)}), s32[64,1,128]{2,1,0:T(1,128)S(1)}, u32[]{:S(2)}, u32[]{:S(2)}) async-start(s32[64,1,128]{2,1,0:T(1,128)} %bitcast.127), calls=%async_computation | async-start | bytes 65536 | tf_op jit(solution)/shard_map/all_to_all | solution.py:44
  53.6 9.2 %copy-start.8 = (s32[1,8192]{1,0:T(1,128)S(1)}, s32[1,8192]{1,0:T(1,128)}, u32[]{:S(2)}) copy-start(s32[1,8192]{1,0:T(1,128)} %param.17) | copy-start | bytes 98308
  53.6 9.3 %copy-start.9 = (bf16[1,16,8192]{2,1,0:T(8,128)(2,1)S(1)}, bf16[1,16,8192]{2,1,0:T(8,128)(2,1)}, u32[]{:S(2)}) copy-start(bf16[1,16,8192]{2,1,0:T(8,128)(2,1)} %param.15) | copy-start | bytes 786436
  53.6 9.3 %copy-start.13 = (bf16[16,64]{1,0:T(8,128)(2,1)S(1)}, bf16[16,64]{1,0:T(8,128)(2,1)}, u32[]{:S(2)}) copy-start(bf16[16,64]{1,0:T(8,128)(2,1)} %param.19) | copy-start | bytes 6148
  56.0 35.6 %all-to-all-start.1 = ((bf16[64,64,128]{2,0,1:T(8,128)(2,1)}), bf16[64,64,128]{2,0,1:T(8,128)(2,1)}, u32[]{:S(2)}, u32[]{:S(2)}) async-start(bf16[64,64,128]{2,0,1:T(8,128)(2,1)} %broadcast_select_fusion), calls=%async_computation.1 | async-start | bytes 2097152 | tf_op jit(solution)/shard_map/all_to_all | solution.py:51
  94.3 49.1 %copy-start.12 = (bf16[64,64]{1,0:T(8,128)(2,1)S(1)}, bf16[64,64]{1,0:T(8,128)(2,1)}, u32[]{:S(2)}) copy-start(bf16[64,64]{1,0:T(8,128)(2,1)} %param.20) | copy-start | bytes 24580
  98.1 46.9 %copy-start.11 = (bf16[64,512]{1,0:T(8,128)(2,1)S(1)}, bf16[64,512]{1,0:T(8,128)(2,1)}, u32[]{:S(2)}) copy-start(bf16[64,512]{1,0:T(8,128)(2,1)} %param.21) | copy-start | bytes 196612
  147.8 1.9 copy-start.16
  147.8 2.3 copy-start.14
  147.9 2.4 copy-start.15
  149.8 3.1 copy-start.20
  152.9 2.3 copy-start.22
  155.2 4.0 copy-start.18
  159.2 1.3 copy-start.4
  160.6 0.7 copy-start.6
  198.2 6.1 copy-start.5
  198.2 34.6 %all-to-all-start.2 = ((bf16[64,64,128]{2,0,1:T(8,128)(2,1)}), bf16[64,64,128]{2,0,1:T(8,128)(2,1)S(1)}, u32[]{:S(2)}, u32[]{:S(2)}) async-start(bf16[64,64,128]{2,0,1:T(8,128)(2,1)} %copy_bitcast_fusion), calls=%async_computation.2 | async-start | bytes 2097152 | tf_op jit(solution)/shard_map/all_to_all | solution.py:83
  204.0 267.5 %all-reduce.7.cloned.1.call-start = ((), (), s32[]{:S(2)}) async-start(), calls=%async_computation.3 | async-start | bytes 4718592 | tf_op jit(solution)/shard_map/psum | solution.py:101
  204.3 1.6 copy-start.21
  206.0 4.0 copy-start.17
  206.0 4.0 copy-start.19
  235.8 44.9 %copy-start.7 = (f32[64,2048]{1,0:T(8,128)S(1)}, f32[64,2048]{1,0:T(8,128)}, u32[]{:S(2)}) copy-start(f32[64,2048]{1,0:T(8,128)} %get-tuple-element.20) | copy-start | bytes 1572868
  283.6 187.9 %copy-start.2 = (f32[64,2048]{0,1:T(8,128)S(1)}, f32[64,2048]{0,1:T(8,128)}, u32[]{:S(2)}) copy-start(f32[64,2048]{0,1:T(8,128)} %scatter_custom_fusion) | copy-start | bytes 1572868
  283.7 189.2 %copy-start.3 = (f32[8192,64]{0,1:T(8,128)S(1)}, f32[8192,64]{0,1:T(8,128)}, u32[]{:S(2)}) copy-start(f32[8192,64]{0,1:T(8,128)} %copy.40) | copy-start | bytes 6291460
  283.7 458.5 %all-reduce.9.cloned.1.call-start = ((), (), s32[]{:S(2)}) async-start(), calls=%async_computation.4 | async-start | bytes 4718592 | tf_op jit(solution)/shard_map/psum | solution.py:100
  472.8 265.1 %copy-start.10 = (bf16[512,64]{0,1:T(8,128)(2,1)S(1)}, bf16[512,64]{0,1:T(8,128)(2,1)}, u32[]{:S(2)}) copy-start(bf16[512,64]{0,1:T(8,128)(2,1)} %param.18) | copy-start | bytes 196612
  745.3 3.2 copy-start.1
Sparse Core Ops, SparseCore 0:
  283.8 187.6 all-reduce.6
  474.1 67.1 all-reduce.8
